TPU v7x, 256 devices: a whole 4x4x8 slice. The times are simulated.
256 devices in a mesh: scen: 16 (over z, x_lo), pt: 16 (over x_hi, y, core).
Axes of the slice: x: 4 (x_hi: 2, x_lo: 2; x = x_hi * 2 + x_lo), y: 4, z: 8, core: 2. Of those that a mesh axis runs over, the one named last changes fastest.
Arguments:
- slip_counts: int32 [2048, 2048], P('scen'), may hold values from 0 to 7
- spectra: bfloat16 [2048, 4, 4096], P('scen', None, 'pt'), may hold values from -0.125 to 0.125
- transfer: bfloat16 [4096, 4, 2048], P('pt', None, 'scen'), may hold values from -0.09375 to 0.09375
- coast_owner: int32 [2048], P('pt'), may hold values from 0 to 127
Outputs:
- coast: bfloat16 [2048, 4, 2048], P('scen', None, 'pt')
- region_energy: float32 [2048, 128], P('scen')
All inputs are finite; a program needn't handle non-finite values.
Results may differ from a plain program's by a relative error of at most 0.015.
Values may be sent and summed in bfloat16 or wider, within the bound.
A program may use at most 64 MiB of HBM per device.

v0:
```python
import jax
import jax.numpy as jnp
from jax import lax
from jax.sharding import PartitionSpec as P

C = 2048
REGIONS = 128
slip_step = 0.25


def coast_block(field_block, trans_block):
    outputs = []
    for freq in range(2):
        field_re = field_block[:, 2 * freq, :]
        field_im = field_block[:, 2 * freq + 1, :]
        real_left = jnp.stack([field_re, -field_im], axis=-1)
        imag_left = jnp.stack([field_im, field_re], axis=-1)
        left_both = jnp.stack([real_left, imag_left], axis=0)
        trans_pair = trans_block[:, 2 * freq : 2 * freq + 2, :]
        product = jnp.einsum(
            "xspc,pcd->sxd", left_both, trans_pair, preferred_element_type=jnp.float32
        )
        outputs.append(product)
    return jnp.concatenate(outputs, axis=1)


def per_device(slip_counts, spectra, transfer, coast_owner):
    weights = (slip_counts.astype(jnp.float32) * slip_step).astype(jnp.bfloat16)
    scen_rows = weights.shape[0]
    comps = spectra.shape[1]
    local_points = spectra.shape[2]
    piece = lax.all_gather(spectra, "scen", axis=0, tiled=True)
    flat_piece = piece.reshape(piece.shape[0], comps * local_points)
    field_sum = jnp.dot(weights, flat_piece, preferred_element_type=jnp.float32)
    field = field_sum.astype(jnp.bfloat16).reshape(scen_rows, comps, local_points)
    trans_whole = lax.all_gather(transfer, "scen", axis=2, tiled=True)
    partial_sum = coast_block(field, trans_whole)
    coast_sum = lax.psum_scatter(
        partial_sum.astype(jnp.bfloat16), "pt", scatter_dimension=2, tiled=True
    ).astype(jnp.float32)
    coast = coast_sum.astype(jnp.bfloat16)
    squares = jnp.sum(coast_sum * coast_sum, axis=1)
    onehot = (coast_owner[:, None] == jnp.arange(REGIONS, dtype=jnp.int32)[None, :]).astype(
        jnp.float32
    )
    local_energy = jnp.dot(
        squares, onehot, precision=lax.Precision.HIGHEST, preferred_element_type=jnp.float32
    )
    energy = lax.psum(local_energy.astype(jnp.bfloat16), "pt").astype(jnp.float32)
    return (coast, energy * (REGIONS / C))


def solution(mesh):
    placed = (P("scen", None), P("scen", None, "pt"), P("pt", None, "scen"), P("pt"))
    return jax.shard_map(
        per_device,
        mesh=mesh,
        in_specs=placed,
        out_specs=(P("scen", None, "pt"), P("scen", None)),
        check_vma=False,
    )
```

profile of v0, /device:TPU:32, one launch (start us, length us, event | category | flops | bytes accessed | tf_op | source)
XLA Modules:
  0.0 396.1 jit_solution(5593497343896343336)
XLA Ops:
  7.2 0.0 all-gather.3.cloned.1.call-start
  7.2 0.7 all-gather.3.cloned.1.call-update
  7.9 0.0 all-gather.5.cloned.1.call-start
  7.9 1.7 copy.14
  9.7 0.0 all-gather.5.cloned.1.call-update
  9.7 0.0 reduce-scatter.4.cloned.1.call-start
  9.7 101.5 %all-gather.3.cloned.1.call-done = bf16[2048,4,256]{2,1,0:T(4,128)(2,1)} async-done(((bf16[128,4,256]{2,1,0:T(4,128)(2,1)}), bf16[2048,4,256]{2,1,0:T(4,128)(2,1)}) %all-gather.3.cloned.1.call-update) | async-done | bytes 4194320 | tf_op jit(solution)/shard_map/all_gather | solution.py:32
  111.2 0.0 copy-start
  111.2 3.3 copy.27
  114.5 0.0 copy-done
  114.5 0.7 convolution_convert_fusion
  115.3 0.2 reshape.32
  115.4 0.4 fusion.17
  115.9 114.5 %all-gather.5.cloned.1.call-done = bf16[256,4,2048]{2,0,1:T(8,128)(2,1)} async-done(((bf16[256,4,128]{2,0,1:T(8,128)(2,1)}), bf16[256,4,2048]{2,0,1:T(8,128)(2,1)}) %all-gather.5.cloned.1.call-update) | async-done | bytes 4194320 | tf_op jit(solution)/shard_map/all_gather | solution.py:36
  230.4 2.3 fusion.3
  232.7 2.3 fusion.2
  235.0 0.2 pad_maximum_fusion
  235.2 2.5 copy.20
  237.8 3.3 copy.36
  241.1 0.0 copy-start.1
  241.1 0.0 reduce-scatter.4.cloned.1.call-update
  241.1 80.7 %reduce-scatter.4.cloned.1.call-done = bf16[128,512]{1,0:T(8,128)(2,1)} async-done(((bf16[2048,512]{1,0:T(8,128)(2,1)}), bf16[128,512]{1,0:T(8,128)(2,1)}) %reduce-scatter.4.cloned.1.call-update) | async-done | bytes 131088
  321.8 0.9 reshape.38
  322.7 0.8 copy.17
  323.5 0.1 copy.21
  323.7 0.0 copy-done.1
  323.7 0.2 convolution_convert_fusion.1
  324.0 65.0 %psum.7 = bf16[128,128]{1,0:T(8,128)(2,1)S(1)} all-reduce(bf16[128,128]{1,0:T(8,128)(2,1)S(1)} %convolution_convert_fusion.1), channel_id=1, replica_groups=mesh['scen'=16,'pt'=16] {'pt'}, use_global_device_ids=true, to_apply=%region_2.0 | all-reduce | flops 16384 | bytes 65536 | tf_op jit(solution)/shard_map/psum | solution.py:49
  388.9 0.6 convert_multiply_fusion
  (5 shorter events, 0.1 us)
Async XLA Ops:
  7.2 104.0 %all-gather.3.cloned.1.call-start = ((), (), s32[]{:S(2)}) async-start(), calls=%async_computation.1 | async-start | bytes 4456448 | tf_op jit(solution)/shard_map/all_gather | solution.py:32
  7.9 222.5 %all-gather.5.cloned.1.call-start = ((), (), s32[]{:S(2)}) async-start(), calls=%async_computation.2 | async-start | bytes 4456448 | tf_op jit(solution)/shard_map/all_gather | solution.py:36
  9.7 312.1 %reduce-scatter.4.cloned.1.call-start = ((), (), s32[]{:S(2)}) async-start(), calls=%async_computation.3 | async-start | bytes 2228224
  111.2 3.3 copy-start
  241.1 82.7 %copy-start.1 = (s32[128]{0:T(128)S(1)}, s32[128]{0:T(128)}, u32[]{:S(2)}) copy-start(s32[128]{0:T(128)} %param.7) | copy-start | bytes 1540
Sparse Core Ops, SparseCore 0:
  9.8 101.3 all-gather.2
  112.9 117.4 all-gather.4
  241.2 80.5 reduce-scatter.3
where the time goes:
time: 396 us
  waiting for transfers between devices  297 us (75%)
  blocking collectives  65 us (16%)
  between operations  13.9 us (4%)
  local copies, waits for them, and re-layouts  13.3 us (3%)
  matrix products  5.58 us (1%)
    all_gather x1, waiting for transfers between devices, per_device(): trans_whole = lax.all_gather(transfer, 'scen', axis=2, tiled=True)  114 us
    all_gather x1, waiting for transfers between devices, per_device(): piece = lax.all_gather(spectra, 'scen', axis=0, tiled=True)  101 us
    unnamed x4, waiting for transfers between devices  81.4 us
    psum x1, blocking collectives, per_device(): lax.psum(local_energy.astype(jnp.bfloat16), 'pt').astype(jnp.float32)  65 us
    unnamed x11, local copies, waits for them, and re-layouts  12.7 us
  transfers between devices with their start and end apart: 3, of which 3 were waited for; matrix products, arithmetic and copies ran while one was open for 2% of the time, Pallas kernels for 0%

commit v1 on v0

--- a/solution.py
+++ b/solution.py
@@ -46,7 +46,13 @@
     local_energy = jnp.dot(
         squares, onehot, precision=lax.Precision.HIGHEST, preferred_element_type=jnp.float32
     )
-    energy = lax.psum(local_energy.astype(jnp.bfloat16), "pt").astype(jnp.float32)
+
+    def spots_search(sheet):
+        val = jax.lax.all_gather(sheet, "pt")
+        q_next = jnp.sum(val, 0)
+        return q_next
+
+    energy = spots_search(local_energy.astype(jnp.bfloat16)).astype(jnp.float32)
     return (coast, energy * (REGIONS / C))
 
 

time: 396 us -> 356 us (0.90)
  blocking collectives: 65 us -> 22.9 us
    psum x1 -> x0, blocking collectives: 65 us -> none  [per_device(): lax.psum(local_energy.astype(jnp.bfloat16), 'pt').astype(jnp.float32)]
    all_gather x0 -> x1, blocking collectives: none -> 22.9 us  [spots_search(): val = jax.lax.all_gather(sheet, 'pt')]
where the time goes in v1:
time: 356 us; the launch traced here: 354 us
  waiting for transfers between devices  297 us (83%)
  blocking collectives  22.9 us (6%)
  between operations  13.9 us (4%)
  local copies, waits for them, and re-layouts  13.3 us (4%)
  matrix products  5.58 us (2%)
    all_gather x1, waiting for transfers between devices, per_device(): trans_whole = lax.all_gather(transfer, 'scen', axis=2, tiled=True)  114 us
    all_gather x1, waiting for transfers between devices, per_device(): piece = lax.all_gather(spectra, 'scen', axis=0, tiled=True)  101 us
    unnamed x4, waiting for transfers between devices  81.4 us
    all_gather x1, blocking collectives, spots_search(): val = jax.lax.all_gather(sheet, 'pt')  22.9 us
    unnamed x11, local copies, waits for them, and re-layouts  12.7 us
  transfers between devices with their start and end apart: 3, of which 3 were waited for; matrix products, arithmetic and copies ran while one was open for 2% of the time, Pallas kernels for 0%

profile of v1, /device:TPU:32, one launch (start us, length us, event | category | flops | bytes accessed | tf_op | source)
XLA Modules:
  0.0 354.1 jit_solution(9042144400755292072)
XLA Ops:
  7.2 0.0 all-gather.4.cloned.1.call-start
  7.2 0.7 all-gather.4.cloned.1.call-update
  7.9 0.0 all-gather.6.cloned.1.call-start
  7.9 1.7 copy.14
  9.7 0.0 all-gather.6.cloned.1.call-update
  9.7 0.0 reduce-scatter.4.cloned.1.call-start
  9.7 101.5 %all-gather.4.cloned.1.call-done = bf16[2048,4,256]{2,1,0:T(4,128)(2,1)} async-done(((bf16[128,4,256]{2,1,0:T(4,128)(2,1)}), bf16[2048,4,256]{2,1,0:T(4,128)(2,1)}) %all-gather.4.cloned.1.call-update) | async-done | bytes 4194320 | tf_op jit(solution)/shard_map/all_gather | solution.py:32
  111.2 0.0 copy-start
  111.2 3.3 copy.27
  114.5 0.0 copy-done
  114.5 0.7 convolution_convert_fusion
  115.3 0.2 reshape.32
  115.4 0.4 fusion.17
  115.9 114.5 %all-gather.6.cloned.1.call-done = bf16[256,4,2048]{2,0,1:T(8,128)(2,1)} async-done(((bf16[256,4,128]{2,0,1:T(8,128)(2,1)}), bf16[256,4,2048]{2,0,1:T(8,128)(2,1)}) %all-gather.6.cloned.1.call-update) | async-done | bytes 4194320 | tf_op jit(solution)/shard_map/all_gather | solution.py:36
  230.4 2.3 fusion.3
  232.7 2.3 fusion.2
  235.0 0.2 pad_maximum_fusion
  235.2 2.5 copy.20
  237.8 3.3 copy.36
  241.1 0.0 copy-start.1
  241.1 0.0 reduce-scatter.4.cloned.1.call-update
  241.1 80.7 %reduce-scatter.4.cloned.1.call-done = bf16[128,512]{1,0:T(8,128)(2,1)} async-done(((bf16[2048,512]{1,0:T(8,128)(2,1)}), bf16[128,512]{1,0:T(8,128)(2,1)}) %reduce-scatter.4.cloned.1.call-update) | async-done | bytes 131088
  321.8 0.9 reshape.39
  322.7 0.8 copy.17
  323.5 0.1 copy.21
  323.7 0.0 copy-done.1
  323.7 0.2 convolution_convert_fusion.1
  324.0 22.9 %all-gather = bf16[2048,128]{1,0:T(8,128)(2,1)S(1)} all-gather(bf16[128,128]{1,0:T(8,128)(2,1)S(1)} %convolution_convert_fusion.1), channel_id=2, replica_groups=mesh['scen'=16,'pt'=16] {'pt'}, dimensions={0}, use_global_device_ids=true | all-gather | bytes 557056 | tf_op jit(solution)/shard_map/all_gather | solution.py:51
  346.9 0.1 reduce_sum.22
  347.0 0.6 convert_multiply_fusion
  (5 shorter events, 0.1 us)
Async XLA Ops:
  7.2 104.0 %all-gather.4.cloned.1.call-start = ((), (), s32[]{:S(2)}) async-start(), calls=%async_computation.1 | async-start | bytes 4456448 | tf_op jit(solution)/shard_map/all_gather | solution.py:32
  7.9 222.5 %all-gather.6.cloned.1.call-start = ((), (), s32[]{:S(2)}) async-start(), calls=%async_computation.2 | async-start | bytes 4456448 | tf_op jit(solution)/shard_map/all_gather | solution.py:36
  9.7 312.1 %reduce-scatter.4.cloned.1.call-start = ((), (), s32[]{:S(2)}) async-start(), calls=%async_computation.3 | async-start | bytes 2228224
  111.2 3.3 copy-start
  241.1 82.7 %copy-start.1 = (s32[128]{0:T(128)S(1)}, s32[128]{0:T(128)}, u32[]{:S(2)}) copy-start(s32[128]{0:T(128)} %param.7) | copy-start | bytes 1540
Sparse Core Ops, SparseCore 0:
  9.8 101.3 all-gather.3
  112.9 117.4 all-gather.5
  241.2 80.5 reduce-scatter.3

commit v2 on v0

--- a/solution.py
+++ b/solution.py
@@ -33,7 +33,8 @@
     flat_piece = piece.reshape(piece.shape[0], comps * local_points)
     field_sum = jnp.dot(weights, flat_piece, preferred_element_type=jnp.float32)
     field = field_sum.astype(jnp.bfloat16).reshape(scen_rows, comps, local_points)
-    trans_whole = lax.all_gather(transfer, "scen", axis=2, tiled=True)
+    outgoing = jnp.stack([transfer] * lax.axis_size("scen"))
+    trans_whole = jnp.concatenate(lax.all_to_all(outgoing, "scen", 0, 0), axis=2)
     partial_sum = coast_block(field, trans_whole)
     coast_sum = lax.psum_scatter(
         partial_sum.astype(jnp.bfloat16), "pt", scatter_dimension=2, tiled=True

time: 396 us -> 349 us (0.88)
  waiting for transfers between devices: 297 us -> 238 us
  starting transfers between devices: 0.12 us -> 9.59 us
  local copies, waits for them, and re-layouts: 13.3 us -> 18.4 us
    all_gather x1 -> x0, waiting for transfers between devices: 114 us -> none  [per_device(): trans_whole = lax.all_gather(transfer, 'scen', axis=2, tiled=True)]
    all_gather x1, waiting for transfers between devices: 101 us -> 158 us  [per_device(): piece = lax.all_gather(spectra, 'scen', axis=0, tiled=True)]
    all_to_all x0 -> x1, starting transfers between devices: none -> 9.51 us  [per_device(): lax.all_to_all(outgoing, 'scen', 0, 0)]
    unnamed x4 -> x3, waiting for transfers between devices: 81.4 us -> 79.8 us
  transfers between devices with their start and end apart: 3 -> 3, of which waited for: 3 -> 2; matrix products, arithmetic and copies ran while one was open for 2% -> 2% of each run, Pallas kernels for 0% -> 0%
where the time goes in v2:
time: 349 us
  waiting for transfers between devices  238 us (68%)
  blocking collectives  65 us (19%)
  local copies, waits for them, and re-layouts  18.4 us (5%)
  between operations  14.2 us (4%)
  starting transfers between devices  9.59 us (3%)
    all_gather x1, waiting for transfers between devices, per_device(): piece = lax.all_gather(spectra, 'scen', axis=0, tiled=True)  158 us
    unnamed x3, waiting for transfers between devices  79.8 us
    psum x1, blocking collectives, per_device(): lax.psum(local_energy.astype(jnp.bfloat16), 'pt').astype(jnp.float32)  65 us
    unnamed x11, local copies, waits for them, and re-layouts  12.1 us
    all_to_all x1, starting transfers between devices, per_device(): lax.all_to_all(outgoing, 'scen', 0, 0)  9.51 us
  transfers between devices with their start and end apart: 3, of which 2 were waited for; matrix products, arithmetic and copies ran while one was open for 2% of the time, Pallas kernels for 0%

profile of v2, /device:TPU:32, one launch (start us, length us, event | category | flops | bytes accessed | tf_op | source)
XLA Modules:
  0.0 348.6 jit_solution(11369902358301048861)
XLA Ops:
  7.2 0.0 all-gather.2.cloned.1.call-start
  7.2 0.7 all-gather.2.cloned.1.call-update
  7.9 1.0 copy.14
  8.9 3.0 stack.27
  11.9 9.5 %all-to-all-start = ((bf16[16,256,4,128]{3,1,2,0:T(8,128)(2,1)}), bf16[16,256,4,128]{3,1,2,0:T(8,128)(2,1)}, u32[]{:S(2)}, u32[]{:S(2)}) async-start(bf16[16,256,4,128]{3,1,2,0:T(8,128)(2,1)} %stack.27), calls=%async_computation | async-start | bytes 8388608 | tf_op jit(solution)/shard_map/all_to_all | solution.py:37
  21.4 0.0 reduce-scatter.4.cloned.1.call-start
  21.4 158.3 %all-gather.2.cloned.1.call-done = bf16[2048,4,256]{2,1,0:T(4,128)(2,1)} async-done(((bf16[128,4,256]{2,1,0:T(4,128)(2,1)}), bf16[2048,4,256]{2,1,0:T(4,128)(2,1)}) %all-gather.2.cloned.1.call-update) | async-done | bytes 4194320 | tf_op jit(solution)/shard_map/all_gather | solution.py:32
  179.8 0.0 copy-start
  179.8 3.3 copy.29
  183.1 0.0 copy-done
  183.1 0.7 convolution_convert_fusion
  183.8 0.2 reshape.40
  184.0 0.4 fusion.17
  184.5 0.0 all-to-all-done
  184.5 2.8 copy_bitcast_fusion
  187.3 0.7 fusion.3
  188.1 0.7 fusion.2
  188.8 0.2 pad_maximum_fusion
  189.0 2.6 copy.21
  191.6 0.0 copy-start.1
  191.6 3.3 copy.39
  194.9 0.0 reduce-scatter.4.cloned.1.call-update
  194.9 79.1 %reduce-scatter.4.cloned.1.call-done = bf16[128,512]{1,0:T(8,128)(2,1)} async-done(((bf16[2048,512]{1,0:T(8,128)(2,1)}), bf16[128,512]{1,0:T(8,128)(2,1)}) %reduce-scatter.4.cloned.1.call-update) | async-done | bytes 131088
  274.0 0.9 reshape.48
  275.0 0.1 copy.22
  275.1 0.8 copy.18
  275.9 0.0 copy-done.1
  276.0 0.2 convolution_convert_fusion.1
  276.2 65.0 %psum.7 = bf16[128,128]{1,0:T(8,128)(2,1)S(1)} all-reduce(bf16[128,128]{1,0:T(8,128)(2,1)S(1)} %convolution_convert_fusion.1), channel_id=1, replica_groups=mesh['scen'=16,'pt'=16] {'pt'}, use_global_device_ids=true, to_apply=%region_2.0 | all-reduce | flops 16384 | bytes 65536 | tf_op jit(solution)/shard_map/psum | solution.py:50
  341.2 0.6 convert_multiply_fusion
  (5 shorter events, 0.1 us)
Async XLA Ops:
  7.2 172.6 %all-gather.2.cloned.1.call-start = ((), (), s32[]{:S(2)}) async-start(), calls=%async_computation.2 | async-start | bytes 4456448 | tf_op jit(solution)/shard_map/all_gather | solution.py:32
  11.9 172.6 %all-to-all-start = ((bf16[16,256,4,128]{3,1,2,0:T(8,128)(2,1)}), bf16[16,256,4,128]{3,1,2,0:T(8,128)(2,1)}, u32[]{:S(2)}, u32[]{:S(2)}) async-start(bf16[16,256,4,128]{3,1,2,0:T(8,128)(2,1)} %stack.27), calls=%async_computation | async-start | bytes 8388608 | tf_op jit(solution)/shard_map/all_to_all | solution.py:37
  21.4 252.6 %reduce-scatter.4.cloned.1.call-start = ((), (), s32[]{:S(2)}) async-start(), calls=%async_computation.3 | async-start | bytes 2228224
  179.8 3.3 copy-start
  191.6 84.4 %copy-start.1 = (s32[128]{0:T(128)S(1)}, s32[128]{0:T(128)}, u32[]{:S(2)}) copy-start(s32[128]{0:T(128)} %param.7) | copy-start | bytes 1540
Sparse Core Ops, SparseCore 0:
  9.8 169.9 all-gather.1
  195.0 78.9 reduce-scatter.3
